TPU v7x, 32 devices: a whole 2x2x4 slice. The times are simulated.
32 devices in a mesh: tm: 8 (over z, x), lev: 4 (over y, core).
Axes of the slice: x: 2, y: 2, z: 4, core: 2. Of those that a mesh axis runs over, the one named last changes fastest.
Arguments:
- fields: bfloat16 [4, 32, 9, 16384], P('lev', 'tm'), may hold values from -18 to 18
- lengths: int32 [8], P('tm'), may hold values from 1 to 4, 24 in all
- owners: int32 [9], replicated, may hold values from 0 to 7, as said below
- thickness: float32 [4], replicated, may hold values from 0.2 to 5
Outputs:
- daily_means: float32 [4, 16, 1, 16384], P('lev', 'tm')
- column_means: float32 [16, 1, 16384], P('tm', None, 'lev')
Inputs may be any that keep to these rules, and one draw needn't show every extreme that they name: `lengths`: the entries sum to 24 and the largest is exactly 4. `owners`: no index owns more than 2 tiles; some index owns exactly 2.
All inputs are finite; a program needn't handle non-finite values. No bound on the sum of `lengths` on one device may be relied on, other than what follows from the above.
Results may differ from a plain program's by a relative error of at most 0.0003.
Values may be sent and summed in bfloat16 or wider, within the bound.
No kernel may reach another device: no remote copies, remote signals or barrier semaphores. Data moves between devices by JAX's collectives and lax.ppermute only.
A program may use at most 128 MiB of HBM per device.

v0:
```python
import jax
import jax.numpy as jnp
from jax import lax
from jax.sharding import PartitionSpec as P

MAXT = 2
HOURS_DEV = 3


def slot_table(owners, slot_total):
    tile_count = owners.shape[0]
    tile_ids = jnp.arange(tile_count, dtype=jnp.int32)
    earlier = (owners[None, :] == owners[:, None]) & (tile_ids[None, :] < tile_ids[:, None])
    tile_rank = jnp.sum(earlier.astype(jnp.int32), axis=1)
    position = owners * MAXT + tile_rank
    slot_ids = jnp.arange(slot_total, dtype=jnp.int32)
    matches = (position[None, :] == slot_ids[:, None]).astype(jnp.int32)
    tile_of = jnp.sum(matches * tile_ids[None, :], axis=1)
    slot_valid = jnp.sum(matches, axis=1)
    return (tile_of, slot_valid)


def local(fields, lengths, owners, thickness):
    local_block = fields[0]
    slot_count = local_block.shape[0]
    devices = lax.axis_size("tm")
    my_index = lax.axis_index("tm")
    all_lengths = lax.all_gather(lengths, "tm", axis=0, tiled=True)
    offsets = jnp.cumsum(all_lengths) - all_lengths
    tile_of, slot_valid = slot_table(owners, devices * MAXT)
    own_slots = lax.dynamic_slice_in_dim(slot_valid, my_index * MAXT, MAXT, 0).astype(jnp.float32)
    day_ids = jnp.arange(devices * HOURS_DEV // 24, dtype=jnp.int32)
    row_ids = jnp.arange(devices * slot_count, dtype=jnp.int32)
    source_ids = row_ids // slot_count
    slot_ids = row_ids % slot_count
    hour_of = offsets[source_ids] + slot_ids
    is_valid = slot_ids < all_lengths[source_ids]
    select = (is_valid[:, None] & (hour_of[:, None] // 24 == day_ids[None, :])).astype(jnp.bfloat16)
    outgoing = jnp.take(local_block, tile_of, axis=1)
    period_means = (
        jnp.einsum(
            "rd,rmc->mdc",
            select,
            lax.all_to_all(outgoing, "tm", split_axis=1, concat_axis=0, tiled=True),
            preferred_element_type=jnp.float32,
        )
        / 24.0
    )
    period_means = period_means * own_slots[:, None, None]
    my_level = lax.axis_index("lev")
    fraction = thickness[my_level] / jnp.sum(thickness)
    weighted = fraction * period_means
    column_sum = lax.psum(weighted, "lev")
    share = column_sum.shape[2] // lax.axis_size("lev")
    column_part = lax.dynamic_slice_in_dim(column_sum, my_level * share, share, 2)
    return (period_means[None], column_part)


def solution(mesh):
    placed = (P("lev", "tm", None, None), P("tm"), P(), P())
    return jax.shard_map(
        local,
        mesh=mesh,
        in_specs=placed,
        out_specs=(P("lev", "tm", None, None), P("tm", None, "lev")),
        check_vma=False,
    )
```

profile of v0, /device:TPU:0, one launch (start us, length us, event | category | flops | bytes accessed | tf_op | source)
XLA Modules:
  0.0 117.4 jit_solution(15610676181587338304)
XLA Ops:
  7.2 0.9 convert_reduce_fusion.1
  8.1 0.7 multiply_add_fusion
  8.8 0.1 convert_reduce_fusion
  8.9 2.4 %gather_fusion = bf16[16,4,16384]{2,1,0:T(4,128)(2,1)S(1)} fusion(bf16[4,9,16384]{2,0,1:T(4,128)(2,1)S(1)} %bitcast.24, s32[1024]{0:T(1024)S(1)} %pad_clamp_fusion.1), kind=kCustom, calls=%fused_computation | custom fusion | bytes 4194368 | tf_op jit(solution)/shard_map/jit(_take)/gather | solution.py:39
  11.3 2.3 %select_bitcast_fusion = bf16[4,16,16384]{2,0,1:T(4,128)(2,1)} fusion(bf16[16,4,16384]{2,1,0:T(4,128)(2,1)S(1)} %gather_fusion, pred[16]{0:T(512)(128)(4,1)S(1)} %compare_and_fusion), kind=kLoop, calls=%fused_computation.5 | loop fusion | flops 1048576 | bytes 4194320 | tf_op jit(solution)/shard_map/jit(_take)/select_n | solution.py:39
  13.7 7.4 %all-to-all-start = ((bf16[4,16,16384]{2,0,1:T(4,128)(2,1)}), bf16[4,16,16384]{2,0,1:T(4,128)(2,1)S(1)}, u32[]{:S(2)}, u32[]{:S(2)}) async-start(bf16[4,16,16384]{2,0,1:T(4,128)(2,1)} %select_bitcast_fusion), calls=%async_computation | async-start | bytes 4194304 | tf_op jit(solution)/shard_map/all_to_all | solution.py:44
  21.1 0.0 all-reduce.3.cloned.1.call-start
  21.8 0.6 dynamic-slice
  22.4 0.8 dynamic-update-slice
  23.1 46.4 %all-reduce = s32[8]{0:T(128)S(1)} all-reduce(s32[8]{0:T(128)S(1)} %dynamic-update-slice), channel_id=1, replica_groups=mesh['tm'=8,'lev'=4] {'tm'}, use_global_device_ids=true, to_apply=%add | all-reduce | flops 8 | bytes 64
  69.5 0.6 dynamic_slice.10
  70.1 0.6 reduce_sum.42
  70.7 0.7 gather_fusion.1
  71.4 0.2 reduce-window.9
  71.6 0.7 gather_fusion.2
  73.6 0.1 convert_multiply_fusion
  73.7 2.2 %copy.7 = bf16[4,8,2,16384]{3,2,0,1:T(2,128)(2,1)S(1)} copy(bf16[4,8,2,16384]{3,0,2,1:T(4,128)(2,1)S(1)} %bitcast.26) | data formatting | bytes 4194304 | tf_op jit(solution)/shard_map/all_to_all | solution.py:44
  75.9 1.3 %fusion = f32[1,2,16384]{2,0,1:T(1,128)S(1)} fusion(bf16[32,2,16384]{2,1,0:T(2,128)(2,1)S(1)} %bitcast.27, s32[32]{0:T(128)S(1)} %gather_fusion.1, s32[32]{0:T(128)S(1)} %gather_fusion.2), kind=kOutput, calls=%fused_computation.3 | convolution fusion | flops 2097728 | bytes 2228480 | tf_op jit(solution)/shard_map/rd,rmc->mdc/dot_general | solution.py:41
  77.2 0.2 broadcast_multiply_fusion
  77.4 0.7 mul.49
  78.1 0.0 all-reduce.3.cloned.1.call-update
  78.1 0.7 broadcast_in_dim.11
  78.9 30.3 %all-reduce.3.cloned.1.call-done = f32[2,1,16384]{2,1,0:T(1,128)} async-done(((f32[2,1,16384]{2,1,0:T(1,128)}), f32[2,1,16384]{2,1,0:T(1,128)}) %all-reduce.3.cloned.1.call-update) | async-done | bytes 131088 | tf_op jit(solution)/shard_map/psum | solution.py:53
  109.2 1.4 %constant_dynamic-slice_fusion = f32[2,1,4096]{2,1,0:T(1,128)} fusion(f32[2,1,16384]{2,1,0:T(1,128)} %all-reduce.3.cloned.1.call-done, s32[]{:T(128)S(6)} %select_n.84), kind=kLoop, calls=%fused_computation.46 | loop fusion | bytes 65540 | tf_op jit(solution)/shard_map/dynamic_slice | solution.py:55
  (14 shorter events, 0.1 us)
Async XLA Ops:
  7.2 1.8 %copy-start = (bf16[1,4,9,16384]{3,1,2,0:T(4,128)(2,1)S(1)}, bf16[1,4,9,16384]{3,1,2,0:T(4,128)(2,1)}, u32[]{:S(2)}) copy-start(bf16[1,4,9,16384]{3,1,2,0:T(4,128)(2,1)} %param.4) | copy-start | bytes 3538948
  13.7 8.1 %copy-start.2 = (u32[32]{0:T(128)S(1)}, u32[32]{0:T(128)}, u32[]{:S(2)}) copy-start(u32[32]{0:T(128)} %constant.88) | copy-start | bytes 388
  13.7 55.8 %copy-start.1 = (f32[4]{0:T(128)S(1)}, f32[4]{0:T(128)}, u32[]{:S(2)}) copy-start(f32[4]{0:T(128)} %param.7) | copy-start | bytes 52
  13.7 60.1 %all-to-all-start = ((bf16[4,16,16384]{2,0,1:T(4,128)(2,1)}), bf16[4,16,16384]{2,0,1:T(4,128)(2,1)S(1)}, u32[]{:S(2)}, u32[]{:S(2)}) async-start(bf16[4,16,16384]{2,0,1:T(4,128)(2,1)} %select_bitcast_fusion), calls=%async_computation | async-start | bytes 4194304 | tf_op jit(solution)/shard_map/all_to_all | solution.py:44
  21.1 88.1 %all-reduce.3.cloned.1.call-start = ((), (), s32[]{:S(2)}) async-start(), calls=%async_computation.1 | async-start | bytes 262144 | tf_op jit(solution)/shard_map/psum | solution.py:53
Sparse Core Ops, SparseCore 0:
  78.3 30.8 all-reduce.2
where the time goes:
time: 118 us; the launch traced here: 117 us
  blocking collectives  46.4 us (39%)
  waiting for transfers between devices  30.3 us (26%)
  between operations  16.1 us (14%)
  local copies, waits for them, and re-layouts  10.7 us (9%)
  starting transfers between devices  7.45 us (6%)
  other arithmetic  5.17 us (4%)
  matrix products  1.25 us (1%)
    unnamed x1, blocking collectives  46.4 us
    psum x1, waiting for transfers between devices, local(): column_sum = lax.psum(weighted, 'lev')  30.3 us
    all_to_all x1, starting transfers between devices, local(): lax.all_to_all(outgoing, 'tm', split_axis=1, concat_axis=0, tiled=True)  7.41 us
    gather x1, local copies, waits for them, and re-layouts, local(): outgoing = jnp.take(local_block, tile_of, axis=1)  2.36 us
  transfers between devices with their start and end apart: 2, of which 1 were waited for; matrix products, arithmetic and copies ran while one was open for 4% of the time, Pallas kernels for 0%

commit v1 on v0

--- a/solution.py
+++ b/solution.py
@@ -50,7 +50,7 @@
     my_level = lax.axis_index("lev")
     fraction = thickness[my_level] / jnp.sum(thickness)
     weighted = fraction * period_means
-    column_sum = lax.psum(weighted, "lev")
+    column_sum = jnp.sum(lax.all_gather(weighted, "lev"), axis=0)
     share = column_sum.shape[2] // lax.axis_size("lev")
     column_part = lax.dynamic_slice_in_dim(column_sum, my_level * share, share, 2)
     return (period_means[None], column_part)

time: 118 us -> 80 us (0.68)
  waiting for transfers between devices: 30.3 us -> 0.01 us
  between operations: 16.1 us -> 2.71 us
  blocking collectives: 46.4 us -> 53.6 us
  local copies, waits for them, and re-layouts: 10.7 us -> 9.33 us
    psum x1 -> x0, waiting for transfers between devices: 30.3 us -> none  [local(): column_sum = lax.psum(weighted, 'lev')]
    all_gather x0 -> x1, blocking collectives: none -> 7.18 us  [local(): column_sum = jnp.sum(lax.all_gather(weighted, 'lev'), axis=0)]
  transfers between devices with their start and end apart: 2 -> 1, of which waited for: 1 -> 0; matrix products, arithmetic and copies ran while one was open for 4% -> 5% of each run, Pallas kernels for 0% -> 0%
where the time goes in v1:
time: 80 us; the launch traced here: 79.7 us
  blocking collectives  53.6 us (67%)
  local copies, waits for them, and re-layouts  9.33 us (12%)
  starting transfers between devices  7.41 us (9%)
  other arithmetic  5.42 us (7%)
  between operations  2.71 us (3%)
  matrix products  1.25 us (2%)
    unnamed x1, blocking collectives  46.4 us
    all_to_all x1, starting transfers between devices, local(): lax.all_to_all(outgoing, 'tm', split_axis=1, concat_axis=0, tiled=True)  7.41 us
    all_gather x1, blocking collectives, local(): column_sum = jnp.sum(lax.all_gather(weighted, 'lev'), axis=0)  7.18 us
    gather x1, local copies, waits for them, and re-layouts, local(): outgoing = jnp.take(local_block, tile_of, axis=1)  2.36 us
    select_n x2, other arithmetic, local(): outgoing = jnp.take(local_block, tile_of, axis=1)  2.35 us
    all_to_all x1, local copies, waits for them, and re-layouts, local(): lax.all_to_all(outgoing, 'tm', split_axis=1, concat_axis=0, tiled=True)  2.18 us
    unnamed x10, local copies, waits for them, and re-layouts  2.15 us
  transfers between devices with their start and end apart: 1, of which 0 were waited for; matrix products, arithmetic and copies ran while one was open for 5% of the time, Pallas kernels for 0%

profile of v1, /device:TPU:0, one launch (start us, length us, event | category | flops | bytes accessed | tf_op | source)
XLA Modules:
  0.0 79.7 jit_solution(5785995772954199772)
XLA Ops:
  0.6 0.0 copy-start
  0.6 0.9 %convert_reduce_fusion.1 = s32[9]{0:T(128)S(1)} fusion(s32[9]{0:T(128)} %param.6), kind=kLoop, calls=%fused_computation.12 | loop fusion | flops 396 | bytes 72 | tf_op jit(solution)/shard_map/reduce_sum | solution.py:14
  1.6 0.7 multiply_add_fusion
  2.3 0.1 convert_reduce_fusion
  2.4 2.4 %gather_fusion = bf16[16,4,16384]{2,1,0:T(4,128)(2,1)S(1)} fusion(bf16[4,9,16384]{2,0,1:T(4,128)(2,1)S(1)} %bitcast.31, s32[1024]{0:T(1024)S(1)} %pad_clamp_fusion.1), kind=kCustom, calls=%fused_computation | custom fusion | bytes 4194368 | tf_op jit(solution)/shard_map/jit(_take)/gather | solution.py:39
  4.8 2.3 %select_bitcast_fusion = bf16[4,16,16384]{2,0,1:T(4,128)(2,1)} fusion(bf16[16,4,16384]{2,1,0:T(4,128)(2,1)S(1)} %gather_fusion, pred[16]{0:T(512)(128)(4,1)S(1)} %compare_and_fusion), kind=kLoop, calls=%fused_computation.5 | loop fusion | flops 1048576 | bytes 4194320 | tf_op jit(solution)/shard_map/jit(_take)/select_n | solution.py:39
  7.1 7.4 %all-to-all-start = ((bf16[4,16,16384]{2,0,1:T(4,128)(2,1)}), bf16[4,16,16384]{2,0,1:T(4,128)(2,1)S(1)}, u32[]{:S(2)}, u32[]{:S(2)}) async-start(bf16[4,16,16384]{2,0,1:T(4,128)(2,1)} %select_bitcast_fusion), calls=%async_computation | async-start | bytes 4194304 | tf_op jit(solution)/shard_map/all_to_all | solution.py:44
  15.2 0.6 dynamic-slice.4
  15.8 0.8 dynamic-update-slice
  16.6 46.4 %all-reduce = s32[8]{0:T(128)S(1)} all-reduce(s32[8]{0:T(128)S(1)} %dynamic-update-slice), channel_id=1, replica_groups=mesh['tm'=8,'lev'=4] {'tm'}, use_global_device_ids=true, to_apply=%add | all-reduce | flops 8 | bytes 64
  63.0 0.7 gather_fusion.1
  63.7 0.2 reduce-window.9
  63.9 0.7 gather_fusion.2
  64.6 0.6 dynamic_slice.10
  65.2 0.6 reduce_sum.51
  67.1 0.1 convert_multiply_fusion
  67.2 0.0 all-to-all-done
  67.2 2.2 %copy.9 = bf16[4,8,2,16384]{3,2,0,1:T(2,128)(2,1)S(1)} copy(bf16[4,8,2,16384]{3,0,2,1:T(4,128)(2,1)S(1)} %bitcast.33) | data formatting | bytes 4194304 | tf_op jit(solution)/shard_map/all_to_all | solution.py:44
  69.4 1.3 %fusion = f32[1,2,16384]{2,0,1:T(1,128)S(1)} fusion(bf16[32,2,16384]{2,1,0:T(2,128)(2,1)S(1)} %bitcast.34, s32[32]{0:T(128)S(1)} %gather_fusion.1, s32[32]{0:T(128)S(1)} %gather_fusion.2), kind=kOutput, calls=%fused_computation.3 | convolution fusion | flops 2097728 | bytes 2228480 | tf_op jit(solution)/shard_map/rd,rmc->mdc/dot_general | solution.py:41
  70.6 0.2 multiply_bitcast_fusion
  70.8 0.8 copy.10
  71.6 7.2 %all-gather.1 = f32[4,2,16384]{2,1,0:T(2,128)S(1)} all-gather(f32[1,2,16384]{2,1,0:T(2,128)S(1)} %get-tuple-element.8), channel_id=2, replica_groups=mesh['tm'=8,'lev'=4] {'lev'}, dimensions={0}, use_global_device_ids=true | all-gather | bytes 655360 | tf_op jit(solution)/shard_map/all_gather | solution.py:53
  78.8 0.3 reduce.1
  79.1 0.6 dynamic_slice.11
  (13 shorter events, 0.1 us)
Async XLA Ops:
  0.6 1.8 %copy-start = (bf16[1,4,9,16384]{3,1,2,0:T(4,128)(2,1)S(1)}, bf16[1,4,9,16384]{3,1,2,0:T(4,128)(2,1)}, u32[]{:S(2)}) copy-start(bf16[1,4,9,16384]{3,1,2,0:T(4,128)(2,1)} %param.4) | copy-start | bytes 3538948
  7.1 8.1 %copy-start.2 = (u32[32]{0:T(128)S(1)}, u32[32]{0:T(128)}, u32[]{:S(2)}) copy-start(u32[32]{0:T(128)} %constant.88) | copy-start | bytes 388
  7.1 57.4 %copy-start.1 = (f32[4]{0:T(128)S(1)}, f32[4]{0:T(128)}, u32[]{:S(2)}) copy-start(f32[4]{0:T(128)} %param.7) | copy-start | bytes 52
  7.1 60.1 %all-to-all-start = ((bf16[4,16,16384]{2,0,1:T(4,128)(2,1)}), bf16[4,16,16384]{2,0,1:T(4,128)(2,1)S(1)}, u32[]{:S(2)}, u32[]{:S(2)}) async-start(bf16[4,16,16384]{2,0,1:T(4,128)(2,1)} %select_bitcast_fusion), calls=%async_computation | async-start | bytes 4194304 | tf_op jit(solution)/shard_map/all_to_all | solution.py:44

commit v2 on v0

--- a/solution.py
+++ b/solution.py
@@ -41,7 +41,12 @@
         jnp.einsum(
             "rd,rmc->mdc",
             select,
-            lax.all_to_all(outgoing, "tm", split_axis=1, concat_axis=0, tiled=True),
+            jnp.concatenate(
+                lax.all_to_all(
+                    jnp.stack(jnp.split(outgoing, lax.axis_size("tm"), axis=1)), "tm", 0, 0
+                ),
+                axis=0,
+            ),
             preferred_element_type=jnp.float32,
         )
         / 24.0

time: 118 us -> 123 us (1.042)
  local copies, waits for them, and re-layouts: 10.7 us -> 17.1 us
  other arithmetic: 5.17 us -> 3.81 us
    unnamed x9 -> x16, local copies, waits for them, and re-layouts: 1.36 us -> 6.94 us
    select_n x2, other arithmetic: 2.35 us -> 1 us  [local(): outgoing = jnp.take(local_block, tile_of, axis=1)]
where the time goes in v2:
time: 123 us; the launch traced here: 122 us
  blocking collectives  46.4 us (38%)
  waiting for transfers between devices  30.3 us (25%)
  local copies, waits for them, and re-layouts  17.1 us (14%)
  between operations  16.1 us (13%)
  starting transfers between devices  7.45 us (6%)
  other arithmetic  3.81 us (3%)
  matrix products  1.25 us (1%)
    unnamed x1, blocking collectives  46.4 us
    psum x1, waiting for transfers between devices, local(): column_sum = lax.psum(weighted, 'lev')  30.3 us
    all_to_all x1, starting transfers between devices, local(): lax.all_to_all(jnp.stack(jnp.split(outgoing, lax.axis_size('tm'), axis=1)...  7.41 us
    unnamed x16, local copies, waits for them, and re-layouts  6.94 us
  transfers between devices with their start and end apart: 2, of which 1 were waited for; matrix products, arithmetic and copies ran while one was open for 4% of the time, Pallas kernels for 0%

profile of v2, /device:TPU:0, one launch (start us, length us, event | category | flops | bytes accessed | tf_op | source)
XLA Modules:
  0.0 122.4 jit_solution(9852250350488496106)
XLA Ops:
  7.2 0.9 convert_reduce_fusion.1
  8.1 0.7 multiply_add_fusion
  8.9 2.4 %gather_fusion = bf16[16,4,16384]{2,1,0:T(4,128)(2,1)S(1)} fusion(bf16[4,9,16384]{2,0,1:T(4,128)(2,1)S(1)} %bitcast.53, s32[1024]{0:T(1024)S(1)} %pad_clamp_fusion.1), kind=kCustom, calls=%fused_computation | custom fusion | bytes 4194368 | tf_op jit(solution)/shard_map/jit(_take)/gather | solution.py:39
  11.3 1.0 select_bitcast_fusion
  12.3 0.8 fusion.9
  13.1 0.8 fusion.8
  13.9 0.8 fusion.7
  14.7 0.8 fusion.6
  15.5 0.8 fusion.5
  16.3 0.8 fusion.4
  17.1 0.8 fusion.3
  17.9 0.8 fusion.2
  18.7 7.4 %all-to-all-start = ((bf16[8,4,2,16384]{3,1,2,0:T(4,128)(2,1)}), bf16[8,4,2,16384]{3,1,2,0:T(4,128)(2,1)S(1)}, u32[]{:S(2)}, u32[]{:S(2)}) async-start(bf16[8,4,2,16384]{3,1,2,0:T(4,128)(2,1)} %fusion.2), calls=%async_computation | async-start | bytes 4194304 | tf_op jit(solution)/shard_map/all_to_all | solution.py:45
  27.4 0.8 dynamic-update-slice
  28.2 46.4 %all-reduce = s32[8]{0:T(128)S(1)} all-reduce(s32[8]{0:T(128)S(1)} %dynamic-update-slice), channel_id=1, replica_groups=mesh['tm'=8,'lev'=4] {'tm'}, use_global_device_ids=true, to_apply=%add | all-reduce | flops 8 | bytes 64
  74.7 0.7 gather_fusion.1
  75.4 0.7 gather_fusion.2
  76.7 0.6 reduce_sum.42
  78.8 2.2 %copy.7 = bf16[8,4,2,16384]{3,2,1,0:T(2,128)(2,1)S(1)} copy(bf16[8,4,2,16384]{3,1,2,0:T(4,128)(2,1)S(1)} %all-to-all-done) | data formatting | bytes 4194304 | tf_op jit(solution)/shard_map/all_to_all | solution.py:45
  80.9 1.3 %fusion = f32[1,2,16384]{2,0,1:T(1,128)S(1)} fusion(bf16[32,2,16384]{2,1,0:T(2,128)(2,1)S(1)} %bitcast.55, s32[32]{0:T(128)S(1)} %gather_fusion.1, s32[32]{0:T(128)S(1)} %gather_fusion.2), kind=kOutput, calls=%fused_computation.3 | convolution fusion | flops 2097728 | bytes 2228480 | tf_op jit(solution)/shard_map/rd,rmc->mdc/dot_general | solution.py:41
  82.4 0.7 mul.49
  83.2 0.7 broadcast_in_dim.11
  83.9 30.3 %all-reduce.3.cloned.1.call-done = f32[2,1,16384]{2,1,0:T(1,128)} async-done(((f32[2,1,16384]{2,1,0:T(1,128)}), f32[2,1,16384]{2,1,0:T(1,128)}) %all-reduce.3.cloned.1.call-update) | async-done | bytes 131088 | tf_op jit(solution)/shard_map/psum | solution.py:58
  114.2 1.4 %constant_dynamic-slice_fusion = f32[2,1,4096]{2,1,0:T(1,128)} fusion(f32[2,1,16384]{2,1,0:T(1,128)} %all-reduce.3.cloned.1.call-done, s32[]{:T(128)S(6)} %select_n.84), kind=kLoop, calls=%fused_computation.62 | loop fusion | bytes 65540 | tf_op jit(solution)/shard_map/dynamic_slice | solution.py:60
  (22 shorter events, 1.9 us)
Async XLA Ops:
  7.2 1.8 %copy-start = (bf16[1,4,9,16384]{3,1,2,0:T(4,128)(2,1)S(1)}, bf16[1,4,9,16384]{3,1,2,0:T(4,128)(2,1)}, u32[]{:S(2)}) copy-start(bf16[1,4,9,16384]{3,1,2,0:T(4,128)(2,1)} %param.4) | copy-start | bytes 3538948
  18.7 8.1 %copy-start.2 = (u32[32]{0:T(128)S(1)}, u32[32]{0:T(128)}, u32[]{:S(2)}) copy-start(u32[32]{0:T(128)} %constant.88) | copy-start | bytes 388
  18.7 57.4 %copy-start.1 = (f32[4]{0:T(128)S(1)}, f32[4]{0:T(128)}, u32[]{:S(2)}) copy-start(f32[4]{0:T(128)} %param.7) | copy-start | bytes 52
  18.7 60.1 %all-to-all-start = ((bf16[8,4,2,16384]{3,1,2,0:T(4,128)(2,1)}), bf16[8,4,2,16384]{3,1,2,0:T(4,128)(2,1)S(1)}, u32[]{:S(2)}, u32[]{:S(2)}) async-start(bf16[8,4,2,16384]{3,1,2,0:T(4,128)(2,1)} %fusion.2), calls=%async_computation | async-start | bytes 4194304 | tf_op jit(solution)/shard_map/all_to_all | solution.py:45
  26.1 88.1 %all-reduce.3.cloned.1.call-start = ((), (), s32[]{:S(2)}) async-start(), calls=%async_computation.1 | async-start | bytes 262144 | tf_op jit(solution)/shard_map/psum | solution.py:58
Sparse Core Ops, SparseCore 0:
  83.3 30.8 all-reduce.2
